TPU v7x, 32 devices: a whole 2x2x4 slice. The times are simulated.
32 devices in a mesh: grp: 8 (over z, core), sp: 4 (over y, x).
Axes of the slice: x: 2, y: 2, z: 4, core: 2. Of those that a mesh axis runs over, the one named last changes fastest.
Arguments:
- acts: bfloat16 [32, 4, 16, 728], P('grp', 'sp'), may hold values from -6 to 6
- cotangent: bfloat16 [32, 4, 16, 728], P(('grp', 'sp')), may hold values from -6 to 6
- depth_kernel: float32 [3, 3, 728], replicated, may hold values from -2 to 2
- point_weight: bfloat16 [728, 728], replicated, may hold values from -0.21875 to 0.21875
- batch_norm_gain: float32 [728], replicated, may hold values from 0.5 to 2
- norm_shift_bias: float32 [728], replicated, may hold values from -1 to 1
Outputs:
- block_out: bfloat16 [32, 4, 16, 728], P(('grp', 'sp'))
- input_grad: bfloat16 [32, 4, 16, 728], P('grp', 'sp')
- weight_grad: float32 [529984], P('sp')
All inputs are finite; a program needn't handle non-finite values.
Results may differ from a plain program's by a relative error of at most 0.018.
Values may be sent and summed in bfloat16 or wider, within the bound.
A program may use at most 64 MiB of HBM per device.

v0:
```python
import jax
import jax.numpy as jnp
from jax import lax
from jax.sharding import PartitionSpec as P


def depth_forward(field, filter_weight):
    rows = field.shape[1]
    cols = field.shape[2]
    padded = jnp.pad(field, ((0, 0), (1, 1), (1, 1), (0, 0)))
    total = jnp.zeros(field.shape, jnp.float32)
    for i in range(3):
        for j in range(3):
            total = total + padded[:, i : i + rows, j : j + cols, :] * filter_weight[i, j]
    return total


def depth_backward(field, filter_weight):
    rows = field.shape[1]
    cols = field.shape[2]
    padded = jnp.pad(field, ((0, 0), (1, 1), (1, 1), (0, 0)))
    total = jnp.zeros(field.shape, jnp.float32)
    for i in range(3):
        for j in range(3):
            total = (
                total
                + padded[:, 2 - i : 2 - i + rows, 2 - j : 2 - j + cols, :] * filter_weight[i, j]
            )
    return total


def body(acts, cotangent, depth_kernel, point_weight, batch_norm_gain, norm_shift_bias):
    channel_count = acts.shape[-1]
    sample_image = lax.all_to_all(acts, "sp", split_axis=0, concat_axis=1, tiled=True)
    input_single_precision = sample_image.astype(jnp.float32)
    hidden = jnp.maximum(input_single_precision, 0.0)
    depthed = depth_forward(hidden, depth_kernel).astype(jnp.bfloat16)
    flat_d = depthed.reshape(-1, channel_count)
    element_count = flat_d.shape[0] * lax.axis_size("sp")
    projected_output = jnp.dot(flat_d, point_weight, preferred_element_type=jnp.float32)
    total, squares = lax.psum(
        (jnp.sum(projected_output, axis=0), jnp.sum(projected_output * projected_output, axis=0)),
        "sp",
    )
    batch_mean = total / element_count
    var = squares / element_count - batch_mean * batch_mean
    inverse_deviation = lax.rsqrt(var + 1e-05)
    normalized_input = (projected_output - batch_mean) * inverse_deviation
    block_out = (
        (
            input_single_precision.reshape(-1, channel_count)
            + batch_norm_gain * normalized_input
            + norm_shift_bias
        )
        .astype(jnp.bfloat16)
        .reshape(sample_image.shape)
    )
    gfloat = cotangent.astype(jnp.float32).reshape(-1, channel_count)
    scaled_output = gfloat * batch_norm_gain
    leading_layer, second_layer = lax.psum(
        (jnp.sum(scaled_output, axis=0), jnp.sum(scaled_output * normalized_input, axis=0)), "sp"
    )
    projected_gradient = (
        inverse_deviation
        * (
            scaled_output
            - leading_layer / element_count
            - normalized_input * (second_layer / element_count)
        )
    ).astype(jnp.bfloat16)
    local_weight = jnp.dot(
        flat_d.T, projected_gradient, preferred_element_type=jnp.float32
    ).reshape(-1)
    ddepth = jnp.dot(
        projected_gradient, point_weight.T, preferred_element_type=jnp.float32
    ).reshape(sample_image.shape)
    dhidden = depth_backward(ddepth, depth_kernel)
    dinput = (
        gfloat.reshape(sample_image.shape) + jnp.where(sample_image > 0, dhidden, 0.0)
    ).astype(jnp.bfloat16)
    input_grad = lax.all_to_all(dinput, "sp", split_axis=1, concat_axis=0, tiled=True)
    slices = lax.psum_scatter(
        local_weight.astype(jnp.bfloat16), "sp", scatter_dimension=0, tiled=True
    ).astype(jnp.float32)
    weight_grad = lax.psum(slices, "grp")
    return (block_out, input_grad, weight_grad)


def solution(mesh):
    in_specs = (P("grp", "sp", None, None), P(("grp", "sp"), None, None, None), P(), P(), P(), P())
    out_specs = (P(("grp", "sp"), None, None, None), P("grp", "sp", None, None), P("sp"))
    return jax.shard_map(body, mesh=mesh, in_specs=in_specs, out_specs=out_specs, check_vma=False)
```

profile of v0, /device:TPU:0, one launch (start us, length us, event | category | flops | bytes accessed | tf_op | source)
XLA Modules:
  0.0 160.6 jit_solution(10437990497592473162)
XLA Ops:
  7.2 5.3 %all-to-all-start = ((bf16[4,1,16,728]{3,2,1,0:T(8,128)(2,1)}), bf16[4,1,16,728]{3,2,1,0:T(8,128)(2,1)S(1)}, u32[]{:S(2)}, u32[]{:S(2)}) async-start(bf16[4,1,16,728]{3,2,1,0:T(8,128)(2,1)} %param.6), calls=%async_computation | async-start | bytes 196608 | tf_op jit(solution)/shard_map/all_to_all | solution.py:34
  12.5 0.0 all-reduce.10.cloned.1.call-start
  12.6 1.0 multiply_reduce_fusion.1
  13.5 1.0 slice_reduce_fusion.8
  14.5 3.0 %all-to-all-done = bf16[4,1,16,728]{3,2,1,0:T(8,128)(2,1)S(1)} async-done(((bf16[4,1,16,728]{3,2,1,0:T(8,128)(2,1)}), bf16[4,1,16,728]{3,2,1,0:T(8,128)(2,1)S(1)}, u32[]{:S(2)}, u32[]{:S(2)}) %all-to-all-start) | async-done | bytes 93216 | tf_op jit(solution)/shard_map/all_to_all | solution.py:34
  17.5 0.1 fusion.9
  17.6 0.3 fusion.39
  18.0 8.4 %all-reduce.4 = (f32[728]{0:T(1024)S(1)}, f32[728]{0:T(1024)S(1)}) all-reduce(f32[728]{0:T(1024)S(1)} %get-tuple-element.7, f32[728]{0:T(1024)S(1)} %get-tuple-element.6), channel_id=1, replica_groups=mesh['grp'=8,'sp'=4] {'sp'}, use_global_device_ids=true, to_apply=%region_3.4 | all-reduce | flops 1456 | bytes 11648 | tf_op jit(solution)/shard_map/psum | solution.py:41
  26.5 0.1 multiply_reduce_fusion
  26.5 9.0 %all-reduce.3 = (f32[728]{0:T(1024)S(1)}, f32[728]{0:T(1024)S(1)}) all-reduce(f32[728]{0:T(1024)S(1)} %multiply_reduce_fusion, f32[728]{0:T(1024)S(1)} %multiply_reduce_fusion.1), channel_id=1, replica_groups=mesh['grp'=8,'sp'=4] {'sp'}, use_global_device_ids=true, to_apply=%region_7.8 | all-reduce | flops 1456 | bytes 11648 | tf_op jit(solution)/shard_map/psum | solution.py:60
  35.6 0.7 multiply_convert_fusion
  36.3 0.5 convolution_convert_fusion
  36.8 3.5 %convert_element_type.59 = bf16[529984]{0:T(1024)(128)(2,1)} reshape(bf16[728,728]{1,0:T(8,128)(2,1)S(1)} %convolution_convert_fusion) | data formatting | bytes 2119936 | tf_op jit(solution)/shard_map/convert_element_type | solution.py:83
  40.3 0.0 all-reduce.10.cloned.1.call-update
  40.3 0.0 all-reduce.8.cloned.1.call-start
  40.3 0.6 dynamic-slice
  41.6 0.5 fusion.40
  42.1 51.5 %all-reduce.10.cloned.1.call-done = bf16[529984]{0:T(1024)(128)(2,1)} async-done(((bf16[529984]{0:T(1024)(128)(2,1)}), bf16[529984]{0:T(1024)(128)(2,1)}) %all-reduce.10.cloned.1.call-update) | async-done | bytes 1059984
  93.5 1.9 %dynamic-slice_convert_fusion = f32[132496]{0:T(1024)} fusion(bf16[529984]{0:T(1024)(128)(2,1)} %all-reduce.10.cloned.1.call-done, u32[]{:T(128)S(6)} %multiply.5), kind=kLoop, calls=%fused_computation.17 | loop fusion | flops 132496 | bytes 794980 | tf_op jit(solution)/shard_map/convert_element_type | solution.py:84
  95.5 0.2 fusion.38
  95.7 7.7 %all_to_all.21 = bf16[1,4,16,728]{3,2,0,1:T(8,128)(2,1)S(1)} all-to-all(bf16[1,4,16,728]{3,2,0,1:T(8,128)(2,1)S(1)} %fusion.38), channel_id=1, replica_groups=mesh['grp'=8,'sp'=4] {'sp'}, dimensions={1} | all-to-all | bytes 186368 | tf_op jit(solution)/shard_map/all_to_all | solution.py:81
  103.4 47.9 %all-reduce.8.cloned.1.call-done = f32[132496]{0:T(1024)} async-done(((f32[132496]{0:T(1024)}), f32[132496]{0:T(1024)}) %all-reduce.8.cloned.1.call-update) | async-done | bytes 530000 | tf_op jit(solution)/shard_map/psum | solution.py:85
  151.3 0.6 copy.16
  151.9 1.9 %copy.17 = f32[132496]{0:T(1024)} copy(f32[132496]{0:T(1024)} %all-reduce.8.cloned.1.call-done) | data formatting | bytes 1059968
  (15 shorter events, 0.1 us)
Async XLA Ops:
  7.2 10.5 %copy-start = (bf16[728,728]{1,0:T(8,128)(2,1)S(1)}, bf16[728,728]{1,0:T(8,128)(2,1)}, u32[]{:S(2)}) copy-start(bf16[728,728]{1,0:T(8,128)(2,1)} %param.9) | copy-start | bytes 3179908
  7.2 10.3 %all-to-all-start = ((bf16[4,1,16,728]{3,2,1,0:T(8,128)(2,1)}), bf16[4,1,16,728]{3,2,1,0:T(8,128)(2,1)S(1)}, u32[]{:S(2)}, u32[]{:S(2)}) async-start(bf16[4,1,16,728]{3,2,1,0:T(8,128)(2,1)} %param.6), calls=%async_computation | async-start | bytes 196608 | tf_op jit(solution)/shard_map/all_to_all | solution.py:34
  12.5 13.9 %copy-start.1 = (bf16[1,4,16,728]{3,2,1,0:T(8,128)(2,1)S(1)}, bf16[1,4,16,728]{3,2,1,0:T(8,128)(2,1)}, u32[]{:S(2)}) copy-start(bf16[1,4,16,728]{3,2,1,0:T(8,128)(2,1)} %param.7) | copy-start | bytes 279556
  12.5 13.9 %copy-start.2 = (f32[728]{0:T(1024)S(1)}, f32[728]{0:T(1024)}, u32[]{:S(2)}) copy-start(f32[728]{0:T(1024)} %param.10) | copy-start | bytes 8740
  12.5 81.0 %all-reduce.10.cloned.1.call-start = ((), (), s32[]{:S(2)}) async-start(), calls=%async_computation.3 | async-start | bytes 2121728
  17.6 18.0 %copy-start.3 = (f32[728]{0:T(1024)S(1)}, f32[728]{0:T(1024)}, u32[]{:S(2)}) copy-start(f32[728]{0:T(1024)} %param.11) | copy-start | bytes 8740
  36.8 3.5 %copy-start.4 = (u32[32]{0:T(128)S(1)}, u32[32]{0:T(128)}, u32[]{:S(2)}) copy-start(u32[32]{0:T(128)} %constant.23) | copy-start | bytes 388
  40.3 111.0 %all-reduce.8.cloned.1.call-start = ((), (), s32[]{:S(2)}) async-start(), calls=%async_computation.2 | async-start | bytes 1064960 | tf_op jit(solution)/shard_map/psum | solution.py:85
Sparse Core Ops, SparseCore 0:
  40.4 53.0 all-reduce.9
  96.5 54.7 all-reduce.7
where the time goes:
time: 161 us
  waiting for transfers between devices  102 us (63%)
  blocking collectives  25.1 us (16%)
  between operations  14.8 us (9%)
  local copies, waits for them, and re-layouts  7.53 us (5%)
  starting transfers between devices  5.41 us (3%)
  other arithmetic  4.04 us (3%)
    unnamed x3, waiting for transfers between devices  51.5 us
    psum x1, waiting for transfers between devices, body(): weight_grad = lax.psum(slices, 'grp')  47.9 us
    psum x1, blocking collectives, body(): lax.psum((jnp.sum(scaled_output, axis=0), jnp.sum(scaled_output * normali...  8.99 us
    psum x1, blocking collectives, body(): lax.psum((jnp.sum(projected_output, axis=0), jnp.sum(projected_output * p...  8.45 us
    all_to_all x1, blocking collectives, body(): lax.all_to_all(dinput, 'sp', split_axis=1, concat_axis=0, tiled=True)  7.68 us
    all_to_all x1, starting transfers between devices, body(): lax.all_to_all(acts, 'sp', split_axis=0, concat_axis=1, tiled=True)  5.34 us
    convert_element_type x1, local copies, waits for them, and re-layouts, body(): local_weight.astype(jnp.bfloat16)  3.46 us
  transfers between devices with their start and end apart: 3, of which 3 were waited for; matrix products, arithmetic and copies ran while one was open for 2% of the time, Pallas kernels for 0%

commit v1 on v0

--- a/solution.py
+++ b/solution.py
@@ -82,7 +82,7 @@
     slices = lax.psum_scatter(
         local_weight.astype(jnp.bfloat16), "sp", scatter_dimension=0, tiled=True
     ).astype(jnp.float32)
-    weight_grad = lax.psum(slices, "grp")
+    weight_grad = jnp.sum(lax.all_gather(slices, "grp"), axis=0)
     return (block_out, input_grad, weight_grad)
 
 

time: 161 us -> 217 us (1.35)
  waiting for transfers between devices: 102 us -> 143 us
  local copies, waits for them, and re-layouts: 7.53 us -> 14.9 us
  other arithmetic: 4.04 us -> 10.7 us
    unnamed x3 -> x4, waiting for transfers between devices: 51.5 us -> 140 us
    psum x1 -> x0, waiting for transfers between devices: 47.9 us -> none  [body(): weight_grad = lax.psum(slices, 'grp')]
    all_gather x0 -> x1, local copies, waits for them, and re-layouts: none -> 6.5 us  [body(): weight_grad = jnp.sum(lax.all_gather(slices, 'grp'), axis=0)]
    reduce_sum x0 -> x1, other arithmetic: none -> 6.23 us  [body(): weight_grad = jnp.sum(lax.all_gather(slices, 'grp'), axis=0)]
    unnamed x0 -> x1, other arithmetic: none -> 2.35 us
where the time goes in v1:
time: 217 us; the launch traced here: 216 us
  waiting for transfers between devices  143 us (66%)
  blocking collectives  25.1 us (12%)
  between operations  15.5 us (7%)
  local copies, waits for them, and re-layouts  14.9 us (7%)
  other arithmetic  10.7 us (5%)
  starting transfers between devices  5.41 us (2%)
    unnamed x4, waiting for transfers between devices  140 us
    psum x1, blocking collectives, body(): lax.psum((jnp.sum(scaled_output, axis=0), jnp.sum(scaled_output * normali...  8.99 us
    psum x1, blocking collectives, body(): lax.psum((jnp.sum(projected_output, axis=0), jnp.sum(projected_output * p...  8.45 us
    all_to_all x1, blocking collectives, body(): lax.all_to_all(dinput, 'sp', split_axis=1, concat_axis=0, tiled=True)  7.68 us
    all_gather x1, local copies, waits for them, and re-layouts, body(): weight_grad = jnp.sum(lax.all_gather(slices, 'grp'), axis=0)  6.5 us
    reduce_sum x1, other arithmetic, body(): weight_grad = jnp.sum(lax.all_gather(slices, 'grp'), axis=0)  6.23 us
    all_to_all x1, starting transfers between devices, body(): lax.all_to_all(acts, 'sp', split_axis=0, concat_axis=1, tiled=True)  5.34 us
  transfers between devices with their start and end apart: 3, of which 3 were waited for; matrix products, arithmetic and copies ran while one was open for 2% of the time, Pallas kernels for 0%

profile of v1, /device:TPU:0, one launch (start us, length us, event | category | flops | bytes accessed | tf_op | source)
XLA Modules:
  0.0 216.2 jit_solution(15554500893325686421)
XLA Ops:
  7.2 5.3 %all-to-all-start = ((bf16[4,1,16,728]{3,2,1,0:T(8,128)(2,1)}), bf16[4,1,16,728]{3,2,1,0:T(8,128)(2,1)S(1)}, u32[]{:S(2)}, u32[]{:S(2)}) async-start(bf16[4,1,16,728]{3,2,1,0:T(8,128)(2,1)} %param.6), calls=%async_computation | async-start | bytes 196608 | tf_op jit(solution)/shard_map/all_to_all | solution.py:34
  12.6 1.0 multiply_reduce_fusion.1
  13.5 0.9 slice_reduce_fusion.8
  14.5 3.0 %all-to-all-done = bf16[4,1,16,728]{3,2,1,0:T(8,128)(2,1)S(1)} async-done(((bf16[4,1,16,728]{3,2,1,0:T(8,128)(2,1)}), bf16[4,1,16,728]{3,2,1,0:T(8,128)(2,1)S(1)}, u32[]{:S(2)}, u32[]{:S(2)}) %all-to-all-start) | async-done | bytes 93216 | tf_op jit(solution)/shard_map/all_to_all | solution.py:34
  17.5 0.1 fusion.9
  17.6 0.3 fusion.39
  18.0 8.4 %all-reduce.5 = (f32[728]{0:T(1024)S(1)}, f32[728]{0:T(1024)S(1)}) all-reduce(f32[728]{0:T(1024)S(1)} %get-tuple-element.10, f32[728]{0:T(1024)S(1)} %get-tuple-element.9), channel_id=1, replica_groups=mesh['grp'=8,'sp'=4] {'sp'}, use_global_device_ids=true, to_apply=%region_3.4 | all-reduce | flops 1456 | bytes 11648 | tf_op jit(solution)/shard_map/psum | solution.py:41
  26.5 0.1 multiply_reduce_fusion
  26.5 9.0 %all-reduce.4 = (f32[728]{0:T(1024)S(1)}, f32[728]{0:T(1024)S(1)}) all-reduce(f32[728]{0:T(1024)S(1)} %multiply_reduce_fusion, f32[728]{0:T(1024)S(1)} %multiply_reduce_fusion.1), channel_id=1, replica_groups=mesh['grp'=8,'sp'=4] {'sp'}, use_global_device_ids=true, to_apply=%region_7.8 | all-reduce | flops 1456 | bytes 11648 | tf_op jit(solution)/shard_map/psum | solution.py:60
  35.6 0.7 multiply_convert_fusion
  36.3 0.5 convolution_convert_fusion
  36.8 3.5 %convert_element_type.57 = bf16[529984]{0:T(1024)(128)(2,1)} reshape(bf16[728,728]{1,0:T(8,128)(2,1)S(1)} %convolution_convert_fusion) | data formatting | bytes 2119936 | tf_op jit(solution)/shard_map/convert_element_type | solution.py:83
  40.4 0.6 dynamic-slice.1
  41.6 0.6 dynamic-slice
  42.8 50.7 %all-reduce.11.cloned.1.call-done = bf16[529984]{0:T(1024)(128)(2,1)} async-done(((bf16[529984]{0:T(1024)(128)(2,1)}), bf16[529984]{0:T(1024)(128)(2,1)}) %all-reduce.11.cloned.1.call-update) | async-done | bytes 1059984
  93.5 2.1 broadcast.72
  95.7 2.3 %convert_dynamic-update-slice_fusion = f32[1059968]{0:T(1024)} fusion(f32[1059968]{0:T(1024)} %broadcast.72, u32[]{:T(128)} %bitcast.11, bf16[529984]{0:T(1024)(128)(2,1)} %all-reduce.11.cloned.1.call-done, u32[]{:T(128)S(6)} %multiply.8), kind=kLoop, calls=%fused_computation.17 | loop fusion | flops 132496 | bytes 799236
  98.1 0.5 fusion.40
  98.5 0.2 fusion.38
  98.7 7.7 %all_to_all.21 = bf16[1,4,16,728]{3,2,0,1:T(8,128)(2,1)S(1)} all-to-all(bf16[1,4,16,728]{3,2,0,1:T(8,128)(2,1)S(1)} %fusion.38), channel_id=1, replica_groups=mesh['grp'=8,'sp'=4] {'sp'}, dimensions={1} | all-to-all | bytes 186368 | tf_op jit(solution)/shard_map/all_to_all | solution.py:81
  106.4 89.6 %all-reduce.9.cloned.1.call-done = f32[1059968]{0:T(1024)} async-done(((f32[1059968]{0:T(1024)}), f32[1059968]{0:T(1024)}) %all-reduce.9.cloned.1.call-update) | async-done | bytes 4239888
  196.0 6.5 %reshape.127 = f32[8,132496]{1,0:T(8,128)} reshape(f32[1059968]{0:T(1024)} %all-reduce.9.cloned.1.call-done) | data formatting | bytes 8479744 | tf_op jit(solution)/shard_map/all_gather | solution.py:85
  202.5 6.2 %reduce_sum.49 = f32[132496]{0:T(1024)} reduce(f32[8,132496]{1,0:T(8,128)} %reshape.127, f32[]{:T(128)} %constant.5.clone.1), dimensions={0}, to_apply=%region_9.10 | reduce | flops 927472 | bytes 4769860 | tf_op jit(solution)/shard_map/reduce_sum | solution.py:85
  208.7 0.6 copy.20
  (20 shorter events, 0.2 us)
Async XLA Ops:
  7.2 10.5 %copy-start = (bf16[728,728]{1,0:T(8,128)(2,1)S(1)}, bf16[728,728]{1,0:T(8,128)(2,1)}, u32[]{:S(2)}) copy-start(bf16[728,728]{1,0:T(8,128)(2,1)} %param.9) | copy-start | bytes 3179908
  7.2 10.3 %all-to-all-start = ((bf16[4,1,16,728]{3,2,1,0:T(8,128)(2,1)}), bf16[4,1,16,728]{3,2,1,0:T(8,128)(2,1)S(1)}, u32[]{:S(2)}, u32[]{:S(2)}) async-start(bf16[4,1,16,728]{3,2,1,0:T(8,128)(2,1)} %param.6), calls=%async_computation | async-start | bytes 196608 | tf_op jit(solution)/shard_map/all_to_all | solution.py:34
  12.5 13.9 %copy-start.1 = (bf16[1,4,16,728]{3,2,1,0:T(8,128)(2,1)S(1)}, bf16[1,4,16,728]{3,2,1,0:T(8,128)(2,1)}, u32[]{:S(2)}) copy-start(bf16[1,4,16,728]{3,2,1,0:T(8,128)(2,1)} %param.7) | copy-start | bytes 279556
  12.5 13.9 %copy-start.2 = (f32[728]{0:T(1024)S(1)}, f32[728]{0:T(1024)}, u32[]{:S(2)}) copy-start(f32[728]{0:T(1024)} %param.10) | copy-start | bytes 8740
  12.5 81.0 %all-reduce.11.cloned.1.call-start = ((), (), s32[]{:S(2)}) async-start(), calls=%async_computation.3 | async-start | bytes 2121728
  17.6 18.0 %copy-start.3 = (f32[728]{0:T(1024)S(1)}, f32[728]{0:T(1024)}, u32[]{:S(2)}) copy-start(f32[728]{0:T(1024)} %param.11) | copy-start | bytes 8740
  36.8 3.6 %copy-start.5 = (u32[32]{0:T(128)S(1)}, u32[32]{0:T(128)}, u32[]{:S(2)}) copy-start(u32[32]{0:T(128)} %constant.29) | copy-start | bytes 388
  36.8 4.8 %copy-start.4 = (u32[32]{0:T(128)S(1)}, u32[32]{0:T(128)}, u32[]{:S(2)}) copy-start(u32[32]{0:T(128)} %constant.23) | copy-start | bytes 388
  40.3 155.7 %all-reduce.9.cloned.1.call-start = ((), (), s32[]{:S(2)}) async-start(), calls=%async_computation.2 | async-start | bytes 8486912
Sparse Core Ops, SparseCore 0:
  40.4 53.0 all-reduce.10
  98.2 97.8 all-reduce.8
